TPU v7x, 32 devices: a whole 2x2x4 slice. The times are simulated.
32 devices in a mesh: rep: 4 (over x, core), fsdp: 8 (over z, y).
Axes of the slice: x: 2, y: 2, z: 4, core: 2. Of those that a mesh axis runs over, the one named last changes fastest.
Arguments:
- tokens: bfloat16 [64, 512, 1024], P('rep', 'fsdp'), may hold values from -6 to 6
- cotangent: bfloat16 [64, 512, 1024], P('rep', 'fsdp'), may hold values from -6 to 6
- lengths: int32 [4, 16], P('rep'), may hold values from 1 to 512, as said below
- deal: int32 [4, 16], P('rep'), may hold values from 0 to 15, each once within a row
- norm_gain: bfloat16 [1024], P('fsdp'), may hold values from 0.099609375 to 1.8984375
- in_weight: bfloat16 [1024, 3072], P('fsdp'), may hold values from -0.1875 to 0.1875
- conv_weight: bfloat16 [1024, 3], P('fsdp'), may hold values from -3 to 3
- out_weight: bfloat16 [1024, 1024], P('fsdp'), may hold values from -0.1875 to 0.1875
- ffn_gain: bfloat16 [1024], P('fsdp'), may hold values from 0.099609375 to 1.8984375
- gate_weight: bfloat16 [1024, 4608], P('fsdp'), may hold values from -0.1875 to 0.1875
- up_weight: bfloat16 [1024, 4608], P('fsdp'), may hold values from -0.1875 to 0.1875
- down_weight: bfloat16 [4608, 1024], P('fsdp'), may hold values from -0.1875 to 0.1875
Outputs:
- block_out: bfloat16 [64, 512, 1024], P('rep', 'fsdp')
- block_grad: bfloat16 [64, 512, 1024], P('rep', 'fsdp')
- norm_gain_grad: float32 [1024], P('fsdp')
- in_grad: float32 [1024, 3072], P('fsdp')
- conv_grad: float32 [1024, 3], P('fsdp')
- out_grad: float32 [1024, 1024], P('fsdp')
- ffn_gain_grad: float32 [1024], P('fsdp')
- gate_grad: float32 [1024, 4608], P('fsdp')
- up_grad: float32 [1024, 4608], P('fsdp')
- down_grad: float32 [4608, 1024], P('fsdp')
Inputs may be any that keep to these rules, and one draw needn't show every extreme that they name: In each row, the 2 lengths of slots 2 i to 2 i + 1 sum to at most 768; in each row one such set sums to exactly 768 and holds a length of exactly 512. `deal`: each row is a permutation of the group's sequence numbers.
All inputs are finite; a program needn't handle non-finite values.
Results may differ from a plain program's by a relative error of at most 0.018.
Values may be sent and summed in bfloat16 or wider, within the bound.
A program may use at most 256 MiB of HBM per device.

v0:
```python
import jax
import jax.numpy as jnp
from jax import lax
from jax.sharding import PartitionSpec as P

EPS = 1e-05
F32 = jnp.float32
BF16 = jnp.bfloat16


def row_scale(values):
    return lax.rsqrt(jnp.mean(values * values, axis=-1, keepdims=True) + EPS)


def norm_back(grad_unit, unit_rows, scale_rows):
    return scale_rows * (
        grad_unit - unit_rows * jnp.mean(grad_unit * unit_rows, axis=-1, keepdims=True)
    )


def over_rows(left_side, right_side):
    return lax.dot_general(
        left_side, right_side, (((0,), (0,)), ((), ())), preferred_element_type=F32
    )


def over_cols(left_side, right_side):
    return lax.dot_general(
        left_side, right_side, (((1,), (1,)), ((), ())), preferred_element_type=F32
    )


def dot(left_side, right_side):
    return jnp.dot(left_side, right_side, preferred_element_type=F32)


def live_mask(lengths, deal, span):
    slots = jnp.arange(deal.shape[1], dtype=jnp.int32)
    picked = deal[0][:, None] == slots[None, :]
    source_len = jnp.sum(jnp.where(picked, lengths[0][:, None], 0), axis=0)
    position = lax.axis_index("fsdp") * span + jnp.arange(span, dtype=jnp.int32)
    return (position[None, :] < source_len[:, None]).astype(F32)[..., None]


def shift(values, amount):
    size = lax.axis_size("fsdp")
    pairs = [(i, i + amount) for i in range(size) if 0 <= i + amount < size]
    return lax.ppermute(values, "fsdp", pairs)


def body(
    tokens,
    cotangent,
    lengths,
    deal,
    norm_gain,
    in_weight,
    conv_weight,
    out_weight,
    ffn_gain,
    gate_weight,
    up_weight,
    down_weight,
):
    seqs, span, width = tokens.shape
    live = live_mask(lengths, deal, span)
    halo = shift(tokens[:, span - 2 :], 1)

    def gather(values):
        return lax.all_gather(values, "fsdp", axis=0, tiled=True)

    norm_gain, in_weight, conv_weight, out_weight = map(
        gather, (norm_gain, in_weight, conv_weight, out_weight)
    )
    ffn_gain, gate_weight, up_weight, down_weight = map(
        gather, (ffn_gain, gate_weight, up_weight, down_weight)
    )
    gain_one = norm_gain.astype(F32)
    gain_two = ffn_gain.astype(F32)
    taps = conv_weight.astype(F32)
    extended = jnp.concatenate([halo, tokens], axis=1).astype(F32)
    scale_ext = row_scale(extended)
    unit_ext = extended * scale_ext
    normed_ext = (unit_ext * gain_one).astype(BF16)
    projected = dot(normed_ext.reshape(-1, width), in_weight).reshape(seqs, span + 2, 3 * width)
    b_gate = projected[:, :, :width]
    c_gate = projected[:, 2:, width : 2 * width]
    x_value = projected[:, :, 2 * width :]
    product = b_gate * x_value
    lags = (product[:, :span], product[:, 1 : span + 1], product[:, 2:])
    convolved = taps[:, 0] * lags[0] + taps[:, 1] * lags[1] + taps[:, 2] * lags[2]
    gated = (c_gate * convolved).astype(BF16).reshape(-1, width)
    token_rows = tokens.astype(F32).reshape(-1, width)
    middle = token_rows + dot(gated, out_weight)
    scale_two = row_scale(middle)
    unit_two = middle * scale_two
    normed_two = (unit_two * gain_two).astype(BF16)
    grad_out = (cotangent.astype(F32) * live).reshape(-1, width)
    grad_ffn = grad_out.astype(BF16)
    gate_lin = dot(normed_two, gate_weight)
    up_lin = dot(normed_two, up_weight)
    sigma = jax.nn.sigmoid(gate_lin)
    hidden = (gate_lin * sigma * up_lin).astype(BF16)
    output = middle + dot(hidden, down_weight)
    down_grad = over_rows(hidden, grad_ffn)
    grad_hidden = over_cols(grad_ffn, down_weight)
    grad_gate = (grad_hidden * up_lin * sigma * (1.0 + gate_lin * (1.0 - sigma))).astype(BF16)
    grad_up = (grad_hidden * gate_lin * sigma).astype(BF16)
    gate_grad = over_rows(normed_two, grad_gate)
    up_grad = over_rows(normed_two, grad_up)
    grad_normed_two = over_cols(grad_gate, gate_weight) + over_cols(grad_up, up_weight)
    ffn_gain_grad = jnp.sum(grad_normed_two * unit_two, axis=0)
    grad_middle = grad_out + norm_back(grad_normed_two * gain_two, unit_two, scale_two)
    grad_mixed = grad_middle.astype(BF16)
    out_grad = over_rows(gated, grad_mixed)
    grad_gated = over_cols(grad_mixed, out_weight).reshape(seqs, span, width)
    grad_c = grad_gated * convolved
    grad_conv = grad_gated * c_gate
    conv_grad = jnp.stack([jnp.sum(grad_conv * lag, axis=(0, 1)) for lag in lags], axis=1)
    ahead = jnp.concatenate([grad_conv, shift(grad_conv[:, :2], -1)], axis=1)
    grad_product = (
        taps[:, 2] * ahead[:, :span]
        + taps[:, 1] * ahead[:, 1 : span + 1]
        + taps[:, 0] * ahead[:, 2:]
    )
    grad_projected = (
        jnp.concatenate(
            [grad_product * x_value[:, 2:], grad_c, grad_product * b_gate[:, 2:]], axis=2
        )
        .astype(BF16)
        .reshape(-1, 3 * width)
    )
    normed_one = normed_ext[:, 2:].reshape(-1, width)
    unit_one = unit_ext[:, 2:].reshape(-1, width)
    scale_one = scale_ext[:, 2:].reshape(-1, 1)
    in_grad = over_rows(normed_one, grad_projected)
    grad_normed_one = over_cols(grad_projected, in_weight)
    norm_gain_grad = jnp.sum(grad_normed_one * unit_one, axis=0)
    grad_tokens = grad_middle + norm_back(grad_normed_one * gain_one, unit_one, scale_one)

    def to_slots(rows):
        return (rows.reshape(seqs, span, width) * live).astype(BF16)

    def reduced(values):
        share = lax.psum_scatter(values.astype(BF16), "fsdp", scatter_dimension=0, tiled=True)
        return lax.psum(share, "rep").astype(F32)

    return (
        to_slots(output),
        to_slots(grad_tokens),
        *map(
            reduced,
            (
                norm_gain_grad,
                in_grad,
                conv_grad,
                out_grad,
                ffn_gain_grad,
                gate_grad,
                up_grad,
                down_grad,
            ),
        ),
    )


def solution(mesh):
    rows = P("rep", "fsdp", None)
    lists = P("rep", None)
    vector = P("fsdp")
    matrix = P("fsdp", None)
    return jax.shard_map(
        body,
        mesh=mesh,
        in_specs=(
            rows,
            rows,
            lists,
            lists,
            vector,
            matrix,
            matrix,
            matrix,
            vector,
            matrix,
            matrix,
            matrix,
        ),
        out_specs=(rows, rows, vector, matrix, matrix, matrix, vector, matrix, matrix, matrix),
        check_vma=False,
    )
```

profile of v0, /device:TPU:0, one launch (start us, length us, event | category | flops | bytes accessed | tf_op | source)
XLA Modules:
  0.0 1513.2 jit_solution(15626529436629893880)
XLA Ops:
  15.6 19.0 %all_gather.26 = bf16[1024,3]{0,1:T(4,128)(2,1)S(1)} all-gather(bf16[128,3]{0,1:T(4,128)(2,1)S(1)} %copy-done.37), channel_id=1, replica_groups=mesh['rep'=4,'fsdp'=8] {'fsdp'}, dimensions={0}, use_global_device_ids=true | all-gather | bytes 6912 | tf_op jit(solution)/shard_map/all_gather | solution.py:70
  39.3 16.4 %all-gather = bf16[8,1,128]{2,1,0:T(2,128)(2,1)S(1)} all-gather(bf16[1,1,128]{2,1,0:T(2,128)(2,1)S(1)} %bitcast.93), channel_id=1, replica_groups=mesh['rep'=4,'fsdp'=8] {'fsdp'}, dimensions={0}, use_global_device_ids=true | all-gather | bytes 2304 | tf_op jit(solution)/shard_map/all_gather | solution.py:70
  55.7 18.4 %all-gather.1 = bf16[8,1,128]{2,1,0:T(2,128)(2,1)S(1)} all-gather(bf16[1,1,128]{2,1,0:T(2,128)(2,1)S(1)} %bitcast.94), channel_id=1, replica_groups=mesh['rep'=4,'fsdp'=8] {'fsdp'}, dimensions={0}, use_global_device_ids=true | all-gather | bytes 2304 | tf_op jit(solution)/shard_map/all_gather | solution.py:70
  75.6 36.5 %all-gather.8.cloned.1.call-done = bf16[1024,3072]{1,0:T(8,128)(2,1)} async-done(((bf16[128,3072]{1,0:T(8,128)(2,1)}), bf16[1024,3072]{1,0:T(8,128)(2,1)}) %all-gather.8.cloned.1.call-update) | async-done | bytes 6291472 | tf_op jit(solution)/shard_map/all_gather | solution.py:70
  112.1 11.4 fusion.11
  133.6 28.2 %all-gather.10.cloned.1.call-done = bf16[1024,1024]{1,0:T(8,128)(2,1)} async-done(((bf16[128,1024]{1,0:T(8,128)(2,1)}), bf16[1024,1024]{1,0:T(8,128)(2,1)}) %all-gather.10.cloned.1.call-update) | async-done | bytes 2097168 | tf_op jit(solution)/shard_map/all_gather | solution.py:70
  168.8 131.7 %all-gather.12.cloned.1.call-done = bf16[1024,4608]{1,0:T(8,128)(2,1)} async-done(((bf16[128,4608]{1,0:T(8,128)(2,1)}), bf16[1024,4608]{1,0:T(8,128)(2,1)}) %all-gather.12.cloned.1.call-update) | async-done | bytes 9437200 | tf_op jit(solution)/shard_map/all_gather | solution.py:70
  300.5 16.1 %fusion.35 = f32[1024,4608]{1,0:T(8,128)} fusion(bf16[1024,1024]{1,0:T(8,128)(2,1)S(1)} %multiply_convert_fusion.7, bf16[1024,4608]{1,0:T(8,128)(2,1)} %all-gather.12.cloned.1.call-done), kind=kOutput, calls=%fused_computation.84 | convolution fusion | flops 9663676416 | bytes 30408704 | tf_op jit(solution)/shard_map/dot_general | solution.py:34
  316.7 122.2 %all-gather.14.cloned.1.call-done = bf16[1024,4608]{1,0:T(8,128)(2,1)} async-done(((bf16[128,4608]{1,0:T(8,128)(2,1)}), bf16[1024,4608]{1,0:T(8,128)(2,1)}) %all-gather.14.cloned.1.call-update) | async-done | bytes 9437200 | tf_op jit(solution)/shard_map/all_gather | solution.py:70
  438.8 17.0 %fusion.36 = f32[1024,4608]{1,0:T(8,128)} fusion(bf16[1024,1024]{1,0:T(8,128)(2,1)} %copy-done.15, bf16[1024,4608]{1,0:T(8,128)(2,1)} %all-gather.14.cloned.1.call-done), kind=kOutput, calls=%fused_computation.85 | convolution fusion | flops 9663676416 | bytes 30408704 | tf_op jit(solution)/shard_map/dot_general | solution.py:34
  455.8 121.3 %all-gather.16.cloned.1.call-done = bf16[4608,1024]{1,0:T(8,128)(2,1)} async-done(((bf16[576,1024]{1,0:T(8,128)(2,1)}), bf16[4608,1024]{1,0:T(8,128)(2,1)}) %all-gather.16.cloned.1.call-update) | async-done | bytes 9437200 | tf_op jit(solution)/shard_map/all_gather | solution.py:70
  577.2 31.1 %multiply_convert_fusion = (bf16[1024,4608]{1,0:T(8,128)(2,1)}, bf16[1024,4608]{1,0:T(8,128)(2,1)}, bf16[1024,4608]{1,0:T(8,128)(2,1)}) fusion(f32[1024,4608]{1,0:T(8,128)} %fusion.35, f32[1024,4608]{1,0:T(8,128)} %fusion.36, bf16[1024,1024]{1,0:T(8,128)(2,1)S(1)} %copy-done.13, bf16[4608,1024]{1,0:T(8,128)(2,1)} %all-gather.16.cloned.1.call-done), kind=kOutput, calls=%fused_computation | convolution fusion | flops 9739173888 | bytes 77594624 | tf_op jit(solution)/shard_map/dot_general | solution.py:28
  608.2 16.1 %fusion.37 = f32[1024,1024]{1,0:T(8,128)} fusion(bf16[1024,4608]{1,0:T(8,128)(2,1)} %get-tuple-element.33, bf16[1024,4608]{1,0:T(8,128)(2,1)} %all-gather.12.cloned.1.call-done), kind=kOutput, calls=%fused_computation.86 | convolution fusion | flops 9663676416 | bytes 23068672 | tf_op jit(solution)/shard_map/dot_general | solution.py:28
  624.3 17.7 %multiply_reduce_fusion = (bf16[1024]{0:T(1024)(128)(2,1)}, f32[1024]{0:T(1024)S(1)}, f32[1024,1024]{1,0:T(8,128)S(1)}) fusion(f32[1024,1024]{1,0:T(8,128)S(1)} %copy-done.7, f32[1024]{0:T(1024)S(1)} %add_rsqrt_fusion.1, f32[1024]{0:T(1024)S(1)} %bitcast.85, f32[1024,1024]{1,0:T(8,128)} %fusion.37, bf16[1024,4608]{1,0:T(8,128)(2,1)} %get-tuple-element.32, ...), kind=kOutput, calls=%fused_computation.49 | convolution fusion | flops 9671014400 | bytes 31471616 | tf_op jit(solution)/shard_map/dot_general | solution.py:28
  647.8 6.0 multiply_reduce_fusion.3
  654.8 6.7 convolution_convert_fusion.3
  679.7 9.4 bitcast_convert_fusion
  689.1 16.4 %convolution_convert_fusion.1 = bf16[1024,4608]{1,0:T(8,128)(2,1)} fusion(bf16[1024,1024]{1,0:T(8,128)(2,1)} %copy-done.15, bf16[1024,4608]{1,0:T(8,128)(2,1)} %get-tuple-element.33), kind=kOutput, calls=%fused_computation.6 | convolution fusion | flops 9668395008 | bytes 20971520 | tf_op jit(solution)/shard_map/dot_general | solution.py:22
  705.6 16.6 %convolution_convert_fusion = bf16[1024,4608]{1,0:T(8,128)(2,1)} fusion(bf16[1024,1024]{1,0:T(8,128)(2,1)} %copy-done.15, bf16[1024,4608]{1,0:T(8,128)(2,1)} %get-tuple-element.32), kind=kOutput, calls=%fused_computation.5 | convolution fusion | flops 9668395008 | bytes 20971520 | tf_op jit(solution)/shard_map/dot_general | solution.py:22
  722.3 16.7 %convolution_convert_fusion.2 = bf16[4608,1024]{1,0:T(8,128)(2,1)} fusion(bf16[1024,4608]{1,0:T(8,128)(2,1)} %get-tuple-element.34, bf16[1024,1024]{1,0:T(8,128)(2,1)} %bitcast_convert_fusion.1), kind=kOutput, calls=%fused_computation.7 | convolution fusion | flops 9668395008 | bytes 20971520 | tf_op jit(solution)/shard_map/dot_general | solution.py:22
  741.0 5.2 slice.92
  746.4 17.6 %convolution_add_fusion.1 = f32[1024,1024]{1,0:T(8,128)} fusion(f32[1024,1024]{1,0:T(8,128)} %copy-done.6, bf16[1024,4608]{1,0:T(8,128)(2,1)} %get-tuple-element.34, bf16[4608,1024]{1,0:T(8,128)(2,1)} %all-gather.16.cloned.1.call-done), kind=kOutput, calls=%fused_computation.66 | convolution fusion | flops 9664724992 | bytes 27262976 | tf_op jit(solution)/shard_map/dot_general | solution.py:34
  764.8 19.7 %reduce-scatter.11.cloned.1.call-done = bf16[128,1024]{1,0:T(8,128)(2,1)} async-done(((bf16[1024,1024]{1,0:T(8,128)(2,1)}), bf16[128,1024]{1,0:T(8,128)(2,1)}) %reduce-scatter.11.cloned.1.call-update) | async-done | bytes 262160 | tf_op jit(solution)/shard_map/reduce_scatter | solution.py:145
  784.5 120.6 %reduce-scatter.9.cloned.1.call-done = bf16[128,3072]{1,0:T(8,128)(2,1)} async-done(((bf16[1024,3072]{1,0:T(8,128)(2,1)}), bf16[128,3072]{1,0:T(8,128)(2,1)}) %reduce-scatter.9.cloned.1.call-update) | async-done | bytes 786448 | tf_op jit(solution)/shard_map/reduce_scatter | solution.py:145
  905.1 166.1 %reduce-scatter.13.cloned.1.call-done = bf16[128,4608]{1,0:T(8,128)(2,1)} async-done(((bf16[1024,4608]{1,0:T(8,128)(2,1)}), bf16[128,4608]{1,0:T(8,128)(2,1)}) %reduce-scatter.13.cloned.1.call-update) | async-done | bytes 1179664 | tf_op jit(solution)/shard_map/reduce_scatter | solution.py:145
  1071.2 165.9 %reduce-scatter.15.cloned.1.call-done = bf16[128,4608]{1,0:T(8,128)(2,1)} async-done(((bf16[1024,4608]{1,0:T(8,128)(2,1)}), bf16[128,4608]{1,0:T(8,128)(2,1)}) %reduce-scatter.15.cloned.1.call-update) | async-done | bytes 1179664 | tf_op jit(solution)/shard_map/reduce_scatter | solution.py:145
  1237.0 166.0 %reduce-scatter.17.cloned.1.call-done = bf16[576,1024]{1,0:T(8,128)(2,1)} async-done(((bf16[4608,1024]{1,0:T(8,128)(2,1)}), bf16[576,1024]{1,0:T(8,128)(2,1)}) %reduce-scatter.17.cloned.1.call-update) | async-done | bytes 1179664 | tf_op jit(solution)/shard_map/reduce_scatter | solution.py:145
  1403.1 12.6 fusion.25
  1415.7 19.4 %all-reduce.2 = (bf16[1024]{0:T(1024)(128)(2,1)S(1)}, bf16[1024]{0:T(1024)(128)(2,1)S(1)}) all-reduce(bf16[1024]{0:T(1024)(128)(2,1)S(1)} %get-tuple-element.15, bf16[1024]{0:T(1024)(128)(2,1)S(1)} %copy-done.36), channel_id=2, replica_groups=mesh['rep'=4,'fsdp'=8] {'fsdp'}, use_global_device_ids=true, to_apply=%region_6.7.clone | all-reduce | flops 2048 | bytes 8192
  1435.3 6.5 all-reduce.3
  1443.5 5.8 fusion.24
  1452.1 45.5 %all-reduce.7.cloned.1.call-done = (bf16[128,3072]{1,0:T(8,128)(2,1)}, bf16[128,1024]{1,0:T(8,128)(2,1)}, bf16[128,4608]{1,0:T(8,128)(2,1)}, bf16[128,4608]{1,0:T(8,128)(2,1)}, bf16[576,1024]{1,0:T(8,128)(2,1)}) async-done(((bf16[128,3072]{1,0:T(8,128)(2,1)}, bf16[128,1024]{1,0:T(8,128)(2,1)}, bf16[128,4608]{1,0:T(8,128)(2,1)}, bf16[128,4608]{1,0:T(8,128)(2,1)}, bf16[576,1024]{1,0:T(8,128)(2,1)}), ...) | async-done | bytes 4587536 | tf_op jit(solution)/shard_map/psum | solution.py:146
  (166 shorter events, 71.7 us)
Async XLA Ops:
  7.2 27.5 %copy-start.42 = (s32[1,16]{1,0:T(1,128)S(1)}, s32[1,16]{1,0:T(1,128)}, u32[]{:S(2)}) copy-start(s32[1,16]{1,0:T(1,128)} %param.15) | copy-start | bytes 196
  7.2 27.4 %copy-start.41 = (s32[1,16]{1,0:T(1,128)S(1)}, s32[1,16]{1,0:T(1,128)}, u32[]{:S(2)}) copy-start(s32[1,16]{1,0:T(1,128)} %param.14) | copy-start | bytes 196
  7.2 104.9 %all-gather.8.cloned.1.call-start = ((), (), s32[]{:S(2)}) async-start(), calls=%async_computation.6 | async-start | bytes 7077888 | tf_op jit(solution)/shard_map/all_gather | solution.py:70
  8.0 153.8 %all-gather.10.cloned.1.call-start = ((), (), s32[]{:S(2)}) async-start(), calls=%async_computation.7 | async-start | bytes 2359296 | tf_op jit(solution)/shard_map/all_gather | solution.py:70
  8.7 291.8 %all-gather.12.cloned.1.call-start = ((), (), s32[]{:S(2)}) async-start(), calls=%async_computation.8 | async-start | bytes 10616832 | tf_op jit(solution)/shard_map/all_gather | solution.py:70
  9.4 429.4 %all-gather.14.cloned.1.call-start = ((), (), s32[]{:S(2)}) async-start(), calls=%async_computation.9 | async-start | bytes 10616832 | tf_op jit(solution)/shard_map/all_gather | solution.py:70
  10.0 567.1 %all-gather.16.cloned.1.call-start = ((), (), s32[]{:S(2)}) async-start(), calls=%async_computation.10 | async-start | bytes 10616832 | tf_op jit(solution)/shard_map/all_gather | solution.py:70
  10.6 753.3 %reduce-scatter.19.cloned.1.call-start = ((), (), s32[]{:S(2)}) async-start(), calls=%async_computation.16 | async-start | bytes 294912
  10.7 63.3 %collective-permute-start = (bf16[16,2,1024]{2,1,0:T(2,128)(2,1)S(1)}, bf16[16,2,1024]{2,1,0:T(2,128)(2,1)S(1)}, u32[]{:S(2)}, u32[]{:S(2)}) collective-permute-start(bf16[16,2,1024]{2,1,0:T(2,128)(2,1)S(1)} %slice.59), channel_id=1, source_target_pairs={{0,1},{1,2},{2,3},{3,4},{4,5},{5,6},{6,7},{8,9},{9,10},{10,11},{11... | collective-permute-start | bytes 196616 | tf_op jit(solution)/shard_map/ppermute | solution.py:48
  37.4 37.7 %copy-start.2 = (f32[16,64,1024]{2,1,0:T(8,128)}, f32[16,64,1024]{2,1,0:T(8,128)S(1)}, u32[]{:S(2)}) copy-start(f32[16,64,1024]{2,1,0:T(8,128)S(1)} %convert_multiply_fusion.2) | copy-start | bytes 12582916
  37.4 18.3 %copy-start.39 = (bf16[128]{0:T(256)(128)(2,1)S(1)}, bf16[128]{0:T(256)(128)(2,1)}, u32[]{:S(2)}) copy-start(bf16[128]{0:T(256)(128)(2,1)} %param.20) | copy-start | bytes 772
  39.2 85.9 %copy-start.27 = (f32[1024,1]{0,1:T(1,128)}, f32[1024,1]{0,1:T(1,128)S(1)}, u32[]{:S(2)}) copy-start(f32[1024,1]{0,1:T(1,128)S(1)} %get-tuple-element.42) | copy-start | bytes 12292
  39.3 85.9 %copy-start.29 = (f32[1024,1]{0,1:T(1,128)}, f32[1024,1]{0,1:T(1,128)S(1)}, u32[]{:S(2)}) copy-start(f32[1024,1]{0,1:T(1,128)S(1)} %get-tuple-element.43) | copy-start | bytes 12292
  39.3 85.9 %copy-start.31 = (f32[1024,1]{0,1:T(1,128)}, f32[1024,1]{0,1:T(1,128)S(1)}, u32[]{:S(2)}) copy-start(f32[1024,1]{0,1:T(1,128)S(1)} %get-tuple-element.44) | copy-start | bytes 12292
  55.7 67.8 %copy-start.25 = (f32[8,1,128]{2,1,0:T(1,128)}, f32[8,1,128]{2,1,0:T(1,128)S(1)}, u32[]{:S(2)}) copy-start(f32[8,1,128]{2,1,0:T(1,128)S(1)} %convert_element_type.136) | copy-start | bytes 12292
  74.1 49.5 %copy-start.20 = (bf16[16,2,1024]{2,1,0:T(2,128)(2,1)}, bf16[16,2,1024]{2,1,0:T(2,128)(2,1)S(1)}, u32[]{:S(2)}) copy-start(bf16[16,2,1024]{2,1,0:T(2,128)(2,1)S(1)} %collective-permute-done) | copy-start | bytes 196612
  75.6 47.9 %copy-start.33 = (f32[16,66]{1,0:T(8,128)}, f32[16,66]{1,0:T(8,128)S(1)}, u32[]{:S(2)}) copy-start(f32[16,66]{1,0:T(8,128)S(1)} %get-tuple-element.41) | copy-start | bytes 12676
  168.8 131.7 %copy-start.15 = (bf16[1024,1024]{1,0:T(8,128)(2,1)}, bf16[1024,1024]{1,0:T(8,128)(2,1)S(1)}, u32[]{:S(2)}) copy-start(bf16[1024,1024]{1,0:T(8,128)(2,1)S(1)} %multiply_convert_fusion.7) | copy-start | bytes 6291460
  316.7 260.5 %copy-start.13 = (bf16[1024,1024]{1,0:T(8,128)(2,1)S(1)}, bf16[1024,1024]{1,0:T(8,128)(2,1)}, u32[]{:S(2)}) copy-start(bf16[1024,1024]{1,0:T(8,128)(2,1)} %bitcast_convert_fusion.1) | copy-start | bytes 6291460
  608.2 16.1 %copy-start.7 = (f32[1024,1024]{1,0:T(8,128)S(1)}, f32[1024,1024]{1,0:T(8,128)}, u32[]{:S(2)}) copy-start(f32[1024,1024]{1,0:T(8,128)} %copy-done.6) | copy-start | bytes 12582916
  624.3 17.7 %copy-start.3 = (f32[16,64,1024]{2,1,0:T(8,128)S(1)}, f32[16,64,1024]{2,1,0:T(8,128)}, u32[]{:S(2)}) copy-start(f32[16,64,1024]{2,1,0:T(8,128)} %copy-done.2) | copy-start | bytes 12582916
  654.7 9.6 copy-start.10
  654.8 9.6 copy-start.21
  654.8 9.6 copy-start.26
  654.8 129.7 %reduce-scatter.11.cloned.1.call-start = ((), (), s32[]{:S(2)}) async-start(), calls=%async_computation.12 | async-start | bytes 2359296 | tf_op jit(solution)/shard_map/reduce_scatter | solution.py:145
  661.6 243.5 %reduce-scatter.9.cloned.1.call-start = ((), (), s32[]{:S(2)}) async-start(), calls=%async_computation.11 | async-start | bytes 7077888 | tf_op jit(solution)/shard_map/reduce_scatter | solution.py:145
  662.8 7.1 collective-permute-start.1
  689.1 382.1 %reduce-scatter.13.cloned.1.call-start = ((), (), s32[]{:S(2)}) async-start(), calls=%async_computation.13 | async-start | bytes 10616832 | tf_op jit(solution)/shard_map/reduce_scatter | solution.py:145
  705.6 531.4 %reduce-scatter.15.cloned.1.call-start = ((), (), s32[]{:S(2)}) async-start(), calls=%async_computation.14 | async-start | bytes 10616832 | tf_op jit(solution)/shard_map/reduce_scatter | solution.py:145
  722.3 680.8 %reduce-scatter.17.cloned.1.call-start = ((), (), s32[]{:S(2)}) async-start(), calls=%async_computation.15 | async-start | bytes 10616832 | tf_op jit(solution)/shard_map/reduce_scatter | solution.py:145
  739.1 758.4 %all-reduce.7.cloned.1.call-start = ((), (), s32[]{:S(2)}) async-start(), calls=%async_computation.17 | async-start | bytes 9175040 | tf_op jit(solution)/shard_map/psum | solution.py:146
  1403.1 12.7 copy-start.36
  (28 other events, 124.7 us)
Sparse Core Ops, SparseCore 0:
  10.2 101.8 all-gather.7
  114.2 47.4 all-gather.9
  163.9 136.5 all-gather.11
  302.6 136.2 all-gather.13
  440.9 136.2 all-gather.15
  654.9 59.4 reduce-scatter.18
  717.9 66.6 reduce-scatter.10
  788.1 116.9 reduce-scatter.8
  908.7 162.4 reduce-scatter.12
  1074.6 162.3 reduce-scatter.14
  1240.6 162.3 reduce-scatter.16
  1405.6 91.8 all-reduce.6
where the time goes:
time: 1520 us; the launch traced here: 1510 us
  waiting for transfers between devices  1130 us (74%)
  matrix products  212 us (14%)
  blocking collectives  79.7 us (5%)
  other arithmetic  49.1 us (3%)
  local copies, waits for them, and re-layouts  20.6 us (1%)
  between operations  15.7 us (1%)
    reduce_scatter x5, waiting for transfers between devices, reduced(): lax.psum_scatter(values.astype(BF16), 'fsdp', scatter_dimension=0, tiled=...  638 us
    all_gather x5, waiting for transfers between devices, gather(): return lax.all_gather(values, 'fsdp', axis=0, tiled=True)  440 us
    dot_general x5, matrix products, over_cols(): lax.dot_general(left_side, right_side, (((1,), (1,)), ((), ())), preferre...  79.8 us
    dot_general x5, matrix products, dot(): return jnp.dot(left_side, right_side, preferred_element_type=F32)  66.7 us
    dot_general x5, matrix products, over_rows(): lax.dot_general(left_side, right_side, (((0,), (0,)), ((), ())), preferre...  65.9 us
    all_gather x3, blocking collectives, gather(): return lax.all_gather(values, 'fsdp', axis=0, tiled=True)  53.8 us
    psum x1, waiting for transfers between devices, reduced(): return lax.psum(share, 'rep').astype(F32)  45.5 us
  transfers between devices with their start and end apart: 14, of which 12 were waited for; matrix products, arithmetic and copies ran while one was open for 12% of the time, Pallas kernels for 0%

commit v1 on v0

--- a/solution.py
+++ b/solution.py
@@ -143,7 +143,7 @@
 
     def reduced(values):
         share = lax.psum_scatter(values.astype(BF16), "fsdp", scatter_dimension=0, tiled=True)
-        return lax.psum(share, "rep").astype(F32)
+        return jnp.sum(lax.all_gather(share, "rep"), axis=0).astype(F32)
 
     return (
         to_slots(output),

time: 1520 us -> 1580 us (1.039)
  waiting for transfers between devices: 1130 us -> 1170 us
    all_gather x0 -> x5, waiting for transfers between devices: none -> 89.1 us  [reduced(): return jnp.sum(lax.all_gather(share, 'rep'), axis=0).astype(F32)]
    reduce_scatter x5, waiting for transfers between devices: 638 us -> 592 us  [reduced(): lax.psum_scatter(values.astype(BF16), 'fsdp', scatter_dimension=0, tiled=...]
    psum x1 -> x0, waiting for transfers between devices: 45.5 us -> none  [reduced(): return lax.psum(share, 'rep').astype(F32)]
    unnamed x13 -> x17, waiting for transfers between devices: 3.23 us -> 43.9 us
  transfers between devices with their start and end apart: 14 -> 18, of which waited for: 12 -> 14; matrix products, arithmetic and copies ran while one was open for 12% -> 13% of each run, Pallas kernels for 0% -> 0%
where the time goes in v1:
time: 1580 us
  waiting for transfers between devices  1170 us (74%)
  matrix products  215 us (14%)
  blocking collectives  88.5 us (6%)
  other arithmetic  64.4 us (4%)
  local copies, waits for them, and re-layouts  19.3 us (1%)
    reduce_scatter x5, waiting for transfers between devices, reduced(): lax.psum_scatter(values.astype(BF16), 'fsdp', scatter_dimension=0, tiled=...  592 us
    all_gather x5, waiting for transfers between devices, gather(): return lax.all_gather(values, 'fsdp', axis=0, tiled=True)  440 us
    all_gather x5, waiting for transfers between devices, reduced(): return jnp.sum(lax.all_gather(share, 'rep'), axis=0).astype(F32)  89.1 us
    dot_general x5, matrix products, over_cols(): lax.dot_general(left_side, right_side, (((1,), (1,)), ((), ())), preferre...  84.8 us
    dot_general x5, matrix products, dot(): return jnp.dot(left_side, right_side, preferred_element_type=F32)  66.5 us
    dot_general x5, matrix products, over_rows(): lax.dot_general(left_side, right_side, (((0,), (0,)), ((), ())), preferre...  63.4 us
    all_gather x3, blocking collectives, gather(): return lax.all_gather(values, 'fsdp', axis=0, tiled=True)  53.7 us
    unnamed x17, waiting for transfers between devices  43.9 us
  transfers between devices with their start and end apart: 18, of which 14 were waited for; matrix products, arithmetic and copies ran while one was open for 13% of the time, Pallas kernels for 0%

profile of v1, /device:TPU:0, one launch (start us, length us, event | category | flops | bytes accessed | tf_op | source)
XLA Modules:
  0.0 1575.2 jit_solution(3971152655006084069)
XLA Ops:
  15.6 19.0 %all_gather.74 = bf16[1024,3]{0,1:T(4,128)(2,1)S(1)} all-gather(bf16[128,3]{0,1:T(4,128)(2,1)S(1)} %copy-done.32), channel_id=1, replica_groups=mesh['rep'=4,'fsdp'=8] {'fsdp'}, dimensions={0}, use_global_device_ids=true | all-gather | bytes 6912 | tf_op jit(solution)/shard_map/all_gather | solution.py:70
  39.3 16.4 %all-gather.8 = bf16[8,1,128]{2,1,0:T(2,128)(2,1)S(1)} all-gather(bf16[1,1,128]{2,1,0:T(2,128)(2,1)S(1)} %bitcast.109), channel_id=1, replica_groups=mesh['rep'=4,'fsdp'=8] {'fsdp'}, dimensions={0}, use_global_device_ids=true | all-gather | bytes 2304 | tf_op jit(solution)/shard_map/all_gather | solution.py:70
  55.6 18.4 %all-gather.9 = bf16[8,1,128]{2,1,0:T(2,128)(2,1)S(1)} all-gather(bf16[1,1,128]{2,1,0:T(2,128)(2,1)S(1)} %bitcast.110), channel_id=1, replica_groups=mesh['rep'=4,'fsdp'=8] {'fsdp'}, dimensions={0}, use_global_device_ids=true | all-gather | bytes 2304 | tf_op jit(solution)/shard_map/all_gather | solution.py:70
  75.6 36.5 %all-gather.23.cloned.1.call-done = bf16[1024,3072]{1,0:T(8,128)(2,1)} async-done(((bf16[128,3072]{1,0:T(8,128)(2,1)}), bf16[1024,3072]{1,0:T(8,128)(2,1)}) %all-gather.23.cloned.1.call-update) | async-done | bytes 6291472 | tf_op jit(solution)/shard_map/all_gather | solution.py:70
  112.1 11.4 fusion.11
  133.5 28.2 %all-gather.25.cloned.1.call-done = bf16[1024,1024]{1,0:T(8,128)(2,1)} async-done(((bf16[128,1024]{1,0:T(8,128)(2,1)}), bf16[1024,1024]{1,0:T(8,128)(2,1)}) %all-gather.25.cloned.1.call-update) | async-done | bytes 2097168 | tf_op jit(solution)/shard_map/all_gather | solution.py:70
  168.8 131.7 %all-gather.27.cloned.1.call-done = bf16[1024,4608]{1,0:T(8,128)(2,1)} async-done(((bf16[128,4608]{1,0:T(8,128)(2,1)}), bf16[1024,4608]{1,0:T(8,128)(2,1)}) %all-gather.27.cloned.1.call-update) | async-done | bytes 9437200 | tf_op jit(solution)/shard_map/all_gather | solution.py:70
  300.5 16.1 %fusion.35 = f32[1024,4608]{1,0:T(8,128)} fusion(bf16[1024,1024]{1,0:T(8,128)(2,1)S(1)} %multiply_convert_fusion.7, bf16[1024,4608]{1,0:T(8,128)(2,1)} %all-gather.27.cloned.1.call-done), kind=kOutput, calls=%fused_computation.86 | convolution fusion | flops 9663676416 | bytes 30408704 | tf_op jit(solution)/shard_map/dot_general | solution.py:34
  316.6 122.2 %all-gather.29.cloned.1.call-done = bf16[1024,4608]{1,0:T(8,128)(2,1)} async-done(((bf16[128,4608]{1,0:T(8,128)(2,1)}), bf16[1024,4608]{1,0:T(8,128)(2,1)}) %all-gather.29.cloned.1.call-update) | async-done | bytes 9437200 | tf_op jit(solution)/shard_map/all_gather | solution.py:70
  438.8 16.9 %fusion.36 = f32[1024,4608]{1,0:T(8,128)} fusion(bf16[1024,1024]{1,0:T(8,128)(2,1)} %copy-done.14, bf16[1024,4608]{1,0:T(8,128)(2,1)} %all-gather.29.cloned.1.call-done), kind=kOutput, calls=%fused_computation.87 | convolution fusion | flops 9663676416 | bytes 30408704 | tf_op jit(solution)/shard_map/dot_general | solution.py:34
  455.8 121.4 %all-gather.31.cloned.1.call-done = bf16[4608,1024]{1,0:T(8,128)(2,1)} async-done(((bf16[576,1024]{1,0:T(8,128)(2,1)}), bf16[4608,1024]{1,0:T(8,128)(2,1)}) %all-gather.31.cloned.1.call-update) | async-done | bytes 9437200 | tf_op jit(solution)/shard_map/all_gather | solution.py:70
  577.2 30.9 %multiply_convert_fusion = (bf16[1024,4608]{1,0:T(8,128)(2,1)}, bf16[1024,4608]{1,0:T(8,128)(2,1)}, bf16[1024,4608]{1,0:T(8,128)(2,1)}) fusion(f32[1024,4608]{1,0:T(8,128)} %fusion.35, f32[1024,4608]{1,0:T(8,128)} %fusion.36, bf16[1024,1024]{1,0:T(8,128)(2,1)S(1)} %copy-done.12, bf16[4608,1024]{1,0:T(8,128)(2,1)} %all-gather.31.cloned.1.call-done), kind=kOutput, calls=%fused_computation | convolution fusion | flops 9739173888 | bytes 77594624 | tf_op jit(solution)/shard_map/dot_general | solution.py:28
  608.0 16.0 %fusion.37 = f32[1024,1024]{1,0:T(8,128)} fusion(bf16[1024,4608]{1,0:T(8,128)(2,1)} %get-tuple-element.25, bf16[1024,4608]{1,0:T(8,128)(2,1)} %all-gather.27.cloned.1.call-done), kind=kOutput, calls=%fused_computation.88 | convolution fusion | flops 9663676416 | bytes 23068672 | tf_op jit(solution)/shard_map/dot_general | solution.py:28
  624.1 17.7 %multiply_reduce_fusion = (bf16[1024]{0:T(1024)(128)(2,1)}, f32[1024]{0:T(1024)S(1)}, f32[1024,1024]{1,0:T(8,128)S(1)}) fusion(f32[1024,1024]{1,0:T(8,128)S(1)} %copy-done.6, f32[1024]{0:T(1024)S(1)} %add_rsqrt_fusion.1, f32[1024]{0:T(1024)S(1)} %bitcast.101, f32[1024,1024]{1,0:T(8,128)} %fusion.37, bf16[1024,4608]{1,0:T(8,128)(2,1)} %get-tuple-element.24, ...), kind=kOutput, calls=%fused_computation.49 | convolution fusion | flops 9671014400 | bytes 31471616 | tf_op jit(solution)/shard_map/dot_general | solution.py:28
  649.1 7.3 fusion.28
  656.5 10.9 multiply_reduce_fusion.3
  680.4 9.5 bitcast_convert_fusion
  689.9 16.4 %convolution_convert_fusion.1 = bf16[1024,4608]{1,0:T(8,128)(2,1)} fusion(bf16[1024,1024]{1,0:T(8,128)(2,1)} %copy-done.14, bf16[1024,4608]{1,0:T(8,128)(2,1)} %get-tuple-element.25), kind=kOutput, calls=%fused_computation.6 | convolution fusion | flops 9668395008 | bytes 20971520 | tf_op jit(solution)/shard_map/dot_general | solution.py:22
  706.4 16.6 %convolution_convert_fusion = bf16[1024,4608]{1,0:T(8,128)(2,1)} fusion(bf16[1024,1024]{1,0:T(8,128)(2,1)} %copy-done.14, bf16[1024,4608]{1,0:T(8,128)(2,1)} %get-tuple-element.24), kind=kOutput, calls=%fused_computation.5 | convolution fusion | flops 9668395008 | bytes 20971520 | tf_op jit(solution)/shard_map/dot_general | solution.py:22
  723.1 17.1 %convolution_convert_fusion.2 = bf16[4608,1024]{1,0:T(8,128)(2,1)} fusion(bf16[1024,4608]{1,0:T(8,128)(2,1)} %get-tuple-element.26, bf16[1024,1024]{1,0:T(8,128)(2,1)} %bitcast_convert_fusion.1), kind=kOutput, calls=%fused_computation.7 | convolution fusion | flops 9668395008 | bytes 20971520 | tf_op jit(solution)/shard_map/dot_general | solution.py:22
  741.9 94.7 %reduce-scatter.9.cloned.1.call-done = bf16[128,3072]{1,0:T(8,128)(2,1)} async-done(((bf16[1024,3072]{1,0:T(8,128)(2,1)}), bf16[128,3072]{1,0:T(8,128)(2,1)}) %reduce-scatter.9.cloned.1.call-update) | async-done | bytes 786448 | tf_op jit(solution)/shard_map/reduce_scatter | solution.py:145
  836.7 166.0 %reduce-scatter.13.cloned.1.call-done = bf16[128,4608]{1,0:T(8,128)(2,1)} async-done(((bf16[1024,4608]{1,0:T(8,128)(2,1)}), bf16[128,4608]{1,0:T(8,128)(2,1)}) %reduce-scatter.13.cloned.1.call-update) | async-done | bytes 1179664 | tf_op jit(solution)/shard_map/reduce_scatter | solution.py:145
  1002.8 166.0 %reduce-scatter.15.cloned.1.call-done = bf16[128,4608]{1,0:T(8,128)(2,1)} async-done(((bf16[1024,4608]{1,0:T(8,128)(2,1)}), bf16[128,4608]{1,0:T(8,128)(2,1)}) %reduce-scatter.15.cloned.1.call-update) | async-done | bytes 1179664 | tf_op jit(solution)/shard_map/reduce_scatter | solution.py:145
  1168.8 165.8 %reduce-scatter.17.cloned.1.call-done = bf16[576,1024]{1,0:T(8,128)(2,1)} async-done(((bf16[4608,1024]{1,0:T(8,128)(2,1)}), bf16[576,1024]{1,0:T(8,128)(2,1)}) %reduce-scatter.17.cloned.1.call-update) | async-done | bytes 1179664 | tf_op jit(solution)/shard_map/reduce_scatter | solution.py:145
  1341.3 17.5 %convolution_add_fusion.1 = f32[1024,1024]{1,0:T(8,128)} fusion(f32[1024,1024]{1,0:T(8,128)} %copy-done.5, bf16[1024,4608]{1,0:T(8,128)(2,1)} %get-tuple-element.26, bf16[4608,1024]{1,0:T(8,128)(2,1)} %all-gather.31.cloned.1.call-done), kind=kOutput, calls=%fused_computation.66 | convolution fusion | flops 9664724992 | bytes 27262976 | tf_op jit(solution)/shard_map/dot_general | solution.py:34
  1358.7 40.1 %reduce-scatter.19.cloned.1.call-done = bf16[128,3]{1,0:T(8,128)(2,1)} async-done(((bf16[1024,3]{1,0:T(8,128)(2,1)}), bf16[128,3]{1,0:T(8,128)(2,1)}) %reduce-scatter.19.cloned.1.call-update) | async-done | bytes 784
  1405.4 12.9 fusion.25
  1418.3 19.6 %all-reduce.2 = (bf16[1024]{0:T(1024)(128)(2,1)S(1)}, bf16[1024]{0:T(1024)(128)(2,1)S(1)}) all-reduce(bf16[1024]{0:T(1024)(128)(2,1)S(1)} %get-tuple-element.15, bf16[1024]{0:T(1024)(128)(2,1)S(1)} %copy-done.31), channel_id=10, replica_groups=mesh['rep'=4,'fsdp'=8] {'fsdp'}, use_global_device_ids=true, to_apply=%region_6.7.clone | all-reduce | flops 2048 | bytes 8192
  1449.2 5.8 fusion.24
  1464.3 20.9 %all-gather.37.cloned.1.call-done = bf16[512,4608]{1,0:T(8,128)(2,1)} async-done(((bf16[128,4608]{1,0:T(8,128)(2,1)}), bf16[512,4608]{1,0:T(8,128)(2,1)}) %all-gather.37.cloned.1.call-update) | async-done | bytes 4718608 | tf_op jit(solution)/shard_map/all_gather | solution.py:146
  1489.9 34.1 %all-gather.39.cloned.1.call-done = bf16[512,4608]{1,0:T(8,128)(2,1)} async-done(((bf16[128,4608]{1,0:T(8,128)(2,1)}), bf16[512,4608]{1,0:T(8,128)(2,1)}) %all-gather.39.cloned.1.call-update) | async-done | bytes 4718608 | tf_op jit(solution)/shard_map/all_gather | solution.py:146
  1528.8 34.1 %all-gather.41.cloned.1.call-done = bf16[2304,1024]{1,0:T(8,128)(2,1)} async-done(((bf16[576,1024]{1,0:T(8,128)(2,1)}), bf16[2304,1024]{1,0:T(8,128)(2,1)}) %all-gather.41.cloned.1.call-update) | async-done | bytes 4718608 | tf_op jit(solution)/shard_map/all_gather | solution.py:146
  (181 shorter events, 101.6 us)
Async XLA Ops:
  7.2 27.5 %copy-start.36 = (s32[1,16]{1,0:T(1,128)S(1)}, s32[1,16]{1,0:T(1,128)}, u32[]{:S(2)}) copy-start(s32[1,16]{1,0:T(1,128)} %param.15) | copy-start | bytes 196
  7.2 27.4 %copy-start.35 = (s32[1,16]{1,0:T(1,128)S(1)}, s32[1,16]{1,0:T(1,128)}, u32[]{:S(2)}) copy-start(s32[1,16]{1,0:T(1,128)} %param.14) | copy-start | bytes 196
  7.2 104.9 %all-gather.23.cloned.1.call-start = ((), (), s32[]{:S(2)}) async-start(), calls=%async_computation.6 | async-start | bytes 7077888 | tf_op jit(solution)/shard_map/all_gather | solution.py:70
  8.0 153.8 %all-gather.25.cloned.1.call-start = ((), (), s32[]{:S(2)}) async-start(), calls=%async_computation.7 | async-start | bytes 2359296 | tf_op jit(solution)/shard_map/all_gather | solution.py:70
  8.7 291.8 %all-gather.27.cloned.1.call-start = ((), (), s32[]{:S(2)}) async-start(), calls=%async_computation.8 | async-start | bytes 10616832 | tf_op jit(solution)/shard_map/all_gather | solution.py:70
  9.4 429.4 %all-gather.29.cloned.1.call-start = ((), (), s32[]{:S(2)}) async-start(), calls=%async_computation.9 | async-start | bytes 10616832 | tf_op jit(solution)/shard_map/all_gather | solution.py:70
  10.0 567.1 %all-gather.31.cloned.1.call-start = ((), (), s32[]{:S(2)}) async-start(), calls=%async_computation.10 | async-start | bytes 10616832 | tf_op jit(solution)/shard_map/all_gather | solution.py:70
  10.6 730.8 %reduce-scatter.11.cloned.1.call-start = ((), (), s32[]{:S(2)}) async-start(), calls=%async_computation.12 | async-start | bytes 2359296 | tf_op jit(solution)/shard_map/reduce_scatter | solution.py:145
  10.7 63.3 %collective-permute-start = (bf16[16,2,1024]{2,1,0:T(2,128)(2,1)S(1)}, bf16[16,2,1024]{2,1,0:T(2,128)(2,1)S(1)}, u32[]{:S(2)}, u32[]{:S(2)}) collective-permute-start(bf16[16,2,1024]{2,1,0:T(2,128)(2,1)S(1)} %slice.59), channel_id=1, source_target_pairs={{0,1},{1,2},{2,3},{3,4},{4,5},{5,6},{6,7},{8,9},{9,10},{10,11},{11... | collective-permute-start | bytes 196616 | tf_op jit(solution)/shard_map/ppermute | solution.py:48
  37.4 37.6 %copy-start.2 = (f32[16,64,1024]{2,1,0:T(8,128)}, f32[16,64,1024]{2,1,0:T(8,128)S(1)}, u32[]{:S(2)}) copy-start(f32[16,64,1024]{2,1,0:T(8,128)S(1)} %convert_multiply_fusion.2) | copy-start | bytes 12582916
  39.2 85.9 %copy-start.22 = (f32[1024,1]{0,1:T(1,128)}, f32[1024,1]{0,1:T(1,128)S(1)}, u32[]{:S(2)}) copy-start(f32[1024,1]{0,1:T(1,128)S(1)} %get-tuple-element.34) | copy-start | bytes 12292
  39.2 85.9 %copy-start.24 = (f32[1024,1]{0,1:T(1,128)}, f32[1024,1]{0,1:T(1,128)S(1)}, u32[]{:S(2)}) copy-start(f32[1024,1]{0,1:T(1,128)S(1)} %get-tuple-element.35) | copy-start | bytes 12292
  39.3 85.9 %copy-start.26 = (f32[1024,1]{0,1:T(1,128)}, f32[1024,1]{0,1:T(1,128)S(1)}, u32[]{:S(2)}) copy-start(f32[1024,1]{0,1:T(1,128)S(1)} %get-tuple-element.36) | copy-start | bytes 12292
  55.6 67.9 %copy-start.20 = (f32[8,1,128]{2,1,0:T(1,128)}, f32[8,1,128]{2,1,0:T(1,128)S(1)}, u32[]{:S(2)}) copy-start(f32[8,1,128]{2,1,0:T(1,128)S(1)} %convert_element_type.152) | copy-start | bytes 12292
  74.0 49.5 %copy-start.16 = (bf16[16,2,1024]{2,1,0:T(2,128)(2,1)}, bf16[16,2,1024]{2,1,0:T(2,128)(2,1)S(1)}, u32[]{:S(2)}) copy-start(bf16[16,2,1024]{2,1,0:T(2,128)(2,1)S(1)} %collective-permute-done) | copy-start | bytes 196612
  75.6 47.9 %copy-start.28 = (f32[16,66]{1,0:T(8,128)}, f32[16,66]{1,0:T(8,128)S(1)}, u32[]{:S(2)}) copy-start(f32[16,66]{1,0:T(8,128)S(1)} %get-tuple-element.33) | copy-start | bytes 12676
  168.8 131.7 %copy-start.14 = (bf16[1024,1024]{1,0:T(8,128)(2,1)}, bf16[1024,1024]{1,0:T(8,128)(2,1)S(1)}, u32[]{:S(2)}) copy-start(bf16[1024,1024]{1,0:T(8,128)(2,1)S(1)} %multiply_convert_fusion.7) | copy-start | bytes 6291460
  316.6 260.5 %copy-start.12 = (bf16[1024,1024]{1,0:T(8,128)(2,1)S(1)}, bf16[1024,1024]{1,0:T(8,128)(2,1)}, u32[]{:S(2)}) copy-start(bf16[1024,1024]{1,0:T(8,128)(2,1)} %bitcast_convert_fusion.1) | copy-start | bytes 6291460
  649.1 187.6 %reduce-scatter.9.cloned.1.call-start = ((), (), s32[]{:S(2)}) async-start(), calls=%async_computation.11 | async-start | bytes 7077888 | tf_op jit(solution)/shard_map/reduce_scatter | solution.py:145
  649.1 25.4 %slice-start = ((s8[14155776]{0:T(1024)(128)(4,1)}), s8[4194304]{0:T(1024)(128)(4,1)S(1)}, s32[]{:S(2)}) async-start(s8[14155776]{0:T(1024)(128)(4,1)} %bitcast.82), calls=%async_computation.22 | async-start | bytes 8388608
  649.1 25.4 %slice-start.1 = ((s8[14155776]{0:T(1024)(128)(4,1)}), s8[4194304]{0:T(1024)(128)(4,1)S(1)}, s32[]{:S(2)}) async-start(s8[14155776]{0:T(1024)(128)(4,1)} %bitcast.82), calls=%async_computation.23 | async-start | bytes 8388608
  667.5 7.0 collective-permute-start.1
  689.9 312.8 %reduce-scatter.13.cloned.1.call-start = ((), (), s32[]{:S(2)}) async-start(), calls=%async_computation.13 | async-start | bytes 10616832 | tf_op jit(solution)/shard_map/reduce_scatter | solution.py:145
  706.4 462.4 %reduce-scatter.15.cloned.1.call-start = ((), (), s32[]{:S(2)}) async-start(), calls=%async_computation.14 | async-start | bytes 10616832 | tf_op jit(solution)/shard_map/reduce_scatter | solution.py:145
  723.1 611.5 %reduce-scatter.17.cloned.1.call-start = ((), (), s32[]{:S(2)}) async-start(), calls=%async_computation.15 | async-start | bytes 10616832 | tf_op jit(solution)/shard_map/reduce_scatter | solution.py:145
  740.3 594.4 %copy-start.37 = (u32[32]{0:T(128)S(1)}, u32[32]{0:T(128)}, u32[]{:S(2)}) copy-start(u32[32]{0:T(128)} %constant.35) | copy-start | bytes 388
  740.3 658.6 %reduce-scatter.19.cloned.1.call-start = ((), (), s32[]{:S(2)}) async-start(), calls=%async_computation.21 | async-start | bytes 294912
  741.3 716.9 %all-gather.35.cloned.1.call-start = ((), (), s32[]{:S(2)}) async-start(), calls=%async_computation.17 | async-start | bytes 1310720 | tf_op jit(solution)/shard_map/all_gather | solution.py:146
  741.9 718.6 %all-gather.33.cloned.1.call-start = ((), (), s32[]{:S(2)}) async-start(), calls=%async_computation.16 | async-start | bytes 3932160 | tf_op jit(solution)/shard_map/all_gather | solution.py:146
  836.7 648.5 %all-gather.37.cloned.1.call-start = ((), (), s32[]{:S(2)}) async-start(), calls=%async_computation.18 | async-start | bytes 5898240 | tf_op jit(solution)/shard_map/all_gather | solution.py:146
  1002.7 521.3 %all-gather.39.cloned.1.call-start = ((), (), s32[]{:S(2)}) async-start(), calls=%async_computation.19 | async-start | bytes 5898240 | tf_op jit(solution)/shard_map/all_gather | solution.py:146
  1168.8 394.2 %all-gather.41.cloned.1.call-start = ((), (), s32[]{:S(2)}) async-start(), calls=%async_computation.20 | async-start | bytes 5898240 | tf_op jit(solution)/shard_map/all_gather | solution.py:146
  (28 other events, 223.0 us)
Sparse Core Ops, SparseCore 0:
  10.2 101.8 all-gather.22
  114.2 47.4 all-gather.24
  163.9 136.5 all-gather.26
  302.6 136.2 all-gather.28
  440.9 136.2 all-gather.30
  649.2 66.8 reduce-scatter.10
  719.7 116.9 reduce-scatter.8
  840.2 162.4 reduce-scatter.12
  1006.3 162.3 reduce-scatter.14
  1172.2 162.3 reduce-scatter.16
  1338.5 60.3 reduce-scatter.18
  1400.3 15.7 all-gather.34
  1417.6 28.5 all-gather.32
  1447.6 37.4 all-gather.36
  1486.5 37.4 all-gather.38
  1525.5 37.4 all-gather.40
